TPU v7x, 32 devices: a whole 2x2x4 slice. The times are simulated.
32 devices in a mesh: row: 8 (over z, y), col: 4 (over x, core).
Axes of the slice: x: 2, y: 2, z: 4, core: 2. Of those that a mesh axis runs over, the one named last changes fastest.
Arguments:
- tokens_in: bfloat16 [192, 8192], P('row', 'col'), may hold values from -6 to 6
- gate_weight: bfloat16 [8192, 28672], P('col', 'row'), may hold values from -0.0625 to 0.0625
- up_weight: bfloat16 [8192, 28672], P('col', 'row'), may hold values from -0.0625 to 0.0625
- down_weight: bfloat16 [28672, 8192], P('row', 'col'), may hold values from -0.03125 to 0.03125
- out_grad: bfloat16 [192, 8192], P('row', 'col'), may hold values from -0.29882812 to 0.29882812
Outputs:
- output: bfloat16 [192, 8192], P('row', 'col')
- in_grad: bfloat16 [192, 8192], P('row', 'col')
- gate_grad: bfloat16 [8192, 28672], P('col', 'row')
- up_grad: bfloat16 [8192, 28672], P('col', 'row')
- down_grad: bfloat16 [28672, 8192], P('row', 'col')
All inputs are finite; a program needn't handle non-finite values.
Results may differ from a plain program's by a relative error of at most 0.0051.
Values may be sent and summed in bfloat16 or wider, within the bound.
A program may use at most 192 MiB of HBM per device.

v0:
```python
import jax
import jax.numpy as jnp
from jax import lax
from jax.sharding import PartitionSpec as P


def contract_last(left, right):
    return lax.dot_general(
        left, right, (((1,), (1,)), ((), ())), preferred_element_type=jnp.float32
    )


def contract_first(left, right):
    return lax.dot_general(
        left, right, (((0,), (0,)), ((), ())), preferred_element_type=jnp.float32
    )


def forward_gate(gate_pre, up_pre):
    sigma_gate = jax.nn.sigmoid(gate_pre)
    activated = gate_pre * sigma_gate
    hidden = (activated * up_pre).astype(jnp.bfloat16)
    return (hidden, sigma_gate, activated)


def backward_gate(d_hidden, gate_pre, up_pre, sigma_gate, activated):
    d_gate = (d_hidden * up_pre * sigma_gate * (1.0 + gate_pre * (1.0 - sigma_gate))).astype(
        jnp.bfloat16
    )
    d_up = (d_hidden * activated).astype(jnp.bfloat16)
    return (d_gate, d_up)


def shards(tokens_in, gate_weight, up_weight, down_weight, out_grad):
    inputs_all = lax.all_gather(tokens_in, "row", axis=0, tiled=True)
    gate_part = jnp.dot(inputs_all, gate_weight, preferred_element_type=jnp.float32)
    up_part = jnp.dot(inputs_all, up_weight, preferred_element_type=jnp.float32)
    gate_pre, up_pre = (
        lax.psum_scatter(gate_part, "col", scatter_dimension=0, tiled=True),
        lax.psum_scatter(up_part, "col", scatter_dimension=0, tiled=True),
    )
    hidden_share, sigma_gate, activated = forward_gate(gate_pre, up_pre)
    hidden_all = lax.all_gather(hidden_share, "col", axis=0, tiled=True)
    output = lax.psum_scatter(
        jnp.dot(hidden_all, down_weight, preferred_element_type=jnp.float32),
        "row",
        scatter_dimension=0,
        tiled=True,
    ).astype(jnp.bfloat16)
    grad_all = lax.all_gather(out_grad, "row", axis=0, tiled=True)
    dhid_part = contract_last(grad_all, down_weight)
    d_hidden = lax.psum_scatter(dhid_part, "col", scatter_dimension=0, tiled=True)
    d_gate, d_up = backward_gate(d_hidden, gate_pre, up_pre, sigma_gate, activated)
    d_gate_all, d_up_all = (
        lax.all_gather(d_gate, "col", axis=0, tiled=True),
        lax.all_gather(d_up, "col", axis=0, tiled=True),
    )
    in_grad = lax.psum_scatter(
        contract_last(d_gate_all, gate_weight) + contract_last(d_up_all, up_weight),
        "row",
        scatter_dimension=0,
        tiled=True,
    ).astype(jnp.bfloat16)
    gate_grad = contract_first(inputs_all, d_gate_all).astype(jnp.bfloat16)
    up_grad = contract_first(inputs_all, d_up_all).astype(jnp.bfloat16)
    down_grad = contract_first(hidden_all, grad_all).astype(jnp.bfloat16)
    return (output, in_grad, gate_grad, up_grad, down_grad)


def solution(mesh):
    in_specs = (P("row", "col"), P("col", "row"), P("col", "row"), P("row", "col"), P("row", "col"))
    out_specs = (
        P("row", "col"),
        P("row", "col"),
        P("col", "row"),
        P("col", "row"),
        P("row", "col"),
    )
    return jax.shard_map(shards, mesh=mesh, in_specs=in_specs, out_specs=out_specs, check_vma=False)
```

profile of v0, /device:TPU:0, one launch (start us, length us, event | category | flops | bytes accessed | tf_op | source)
XLA Modules:
  0.0 378.7 jit_solution(6762438291876996533)
XLA Ops:
  7.2 34.1 %all_gather.17 = bf16[192,2048]{1,0:T(8,128)(2,1)S(1)} all-gather(bf16[24,2048]{1,0:T(8,128)(2,1)} %param.9), channel_id=1, replica_groups=mesh['row'=8,'col'=4] {'row'}, dimensions={0}, use_global_device_ids=true | all-gather | bytes 884736 | tf_op jit(solution)/shard_map/all_gather | solution.py:50
  41.3 11.7 %fusion.6 = f32[192,3584]{1,0:T(8,128)} fusion(bf16[192,2048]{1,0:T(8,128)(2,1)S(1)} %all_gather.17, bf16[3584,2048]{1,0:T(8,128)(2,1)} %param.8), kind=kOutput, calls=%fused_computation.14 | convolution fusion | flops 2818572288 | bytes 18219008 | tf_op jit(solution)/shard_map/dot_general | solution.py:8
  53.0 0.0 reduce-scatter.6.cloned.1.call-start
  53.1 0.8 copy-done.3
  53.9 32.1 %all_gather.15 = bf16[192,2048]{1,0:T(8,128)(2,1)S(1)} all-gather(bf16[24,2048]{1,0:T(8,128)(2,1)S(1)} %copy-done.3), channel_id=1, replica_groups=mesh['row'=8,'col'=4] {'row'}, dimensions={0}, use_global_device_ids=true | all-gather | bytes 884736 | tf_op jit(solution)/shard_map/all_gather | solution.py:35
  86.0 9.8 %fusion.3 = f32[192,3584]{1,0:T(8,128)} fusion(bf16[192,2048]{1,0:T(8,128)(2,1)S(1)} %all_gather.15, bf16[2048,3584]{1,0:T(8,128)(2,1)} %param.6), kind=kOutput, calls=%fused_computation.11 | convolution fusion | flops 2818572288 | bytes 18219008 | tf_op jit(solution)/shard_map/dot_general | solution.py:36
  95.8 0.0 reduce-scatter.8.cloned.1.call-start
  95.8 9.7 %fusion.4 = f32[192,3584]{1,0:T(8,128)} fusion(bf16[192,2048]{1,0:T(8,128)(2,1)S(1)} %all_gather.15, bf16[2048,3584]{1,0:T(8,128)(2,1)} %param.7), kind=kOutput, calls=%fused_computation.12 | convolution fusion | flops 2818572288 | bytes 18219008 | tf_op jit(solution)/shard_map/dot_general | solution.py:37
  105.6 0.0 all-gather.4.cloned.1.call-start
  105.6 26.5 %reduce-scatter.6.cloned.1.call-done = f32[48,3584]{1,0:T(8,128)} async-done(((f32[192,3584]{1,0:T(8,128)}), f32[48,3584]{1,0:T(8,128)}) %reduce-scatter.6.cloned.1.call-update) | async-done | bytes 688144 | tf_op jit(solution)/shard_map/reduce_scatter | solution.py:39
  132.1 38.5 %reduce-scatter.8.cloned.1.call-done = f32[48,3584]{1,0:T(8,128)} async-done(((f32[192,3584]{1,0:T(8,128)}), f32[48,3584]{1,0:T(8,128)}) %reduce-scatter.8.cloned.1.call-update) | async-done | bytes 688144 | tf_op jit(solution)/shard_map/reduce_scatter | solution.py:40
  170.7 2.8 multiply_convert_fusion
  173.5 0.0 all-gather.6.cloned.1.call-start
  173.5 0.5 all-gather.6.cloned.1.call-update
  174.1 0.5 all-gather.8.cloned.1.call-update
  174.6 0.0 reduce-scatter.10.cloned.1.call-start
  174.7 17.5 %all-gather.4.cloned.1.call-done = bf16[192,3584]{1,0:T(8,128)(2,1)} async-done(((bf16[48,3584]{1,0:T(8,128)(2,1)}), bf16[192,3584]{1,0:T(8,128)(2,1)}) %all-gather.4.cloned.1.call-update) | async-done | bytes 1376272 | tf_op jit(solution)/shard_map/all_gather | solution.py:43
  192.2 9.8 %fusion.5 = f32[192,2048]{1,0:T(8,128)} fusion(bf16[192,3584]{1,0:T(8,128)(2,1)} %all-gather.4.cloned.1.call-done, bf16[3584,2048]{1,0:T(8,128)(2,1)} %param.8), kind=kOutput, calls=%fused_computation.13 | convolution fusion | flops 2818572288 | bytes 17629184 | tf_op jit(solution)/shard_map/dot_general | solution.py:45
  202.0 0.2 reduce-scatter.14.cloned.1.call-start
  202.2 10.5 %all-gather.6.cloned.1.call-done = bf16[192,3584]{1,0:T(8,128)(2,1)} async-done(((bf16[48,3584]{1,0:T(8,128)(2,1)}), bf16[192,3584]{1,0:T(8,128)(2,1)}) %all-gather.6.cloned.1.call-update) | async-done | bytes 1376272 | tf_op jit(solution)/shard_map/all_gather | solution.py:55
  212.7 8.5 %fusion.7 = f32[192,2048]{1,0:T(8,128)S(1)} fusion(bf16[192,3584]{1,0:T(8,128)(2,1)} %all-gather.6.cloned.1.call-done, bf16[2048,3584]{1,0:T(8,128)(2,1)} %param.6), kind=kOutput, calls=%fused_computation.15 | convolution fusion | flops 2818572288 | bytes 17629184 | tf_op jit(solution)/shard_map/dot_general | solution.py:8
  221.2 12.1 %all-gather.8.cloned.1.call-done = bf16[192,3584]{1,0:T(8,128)(2,1)} async-done(((bf16[48,3584]{1,0:T(8,128)(2,1)}), bf16[192,3584]{1,0:T(8,128)(2,1)}) %all-gather.8.cloned.1.call-update) | async-done | bytes 1376272 | tf_op jit(solution)/shard_map/all_gather | solution.py:56
  233.3 11.6 %convolution_add_fusion = f32[192,2048]{1,0:T(8,128)} fusion(f32[192,2048]{1,0:T(8,128)S(1)} %fusion.7, bf16[192,3584]{1,0:T(8,128)(2,1)} %all-gather.8.cloned.1.call-done, bf16[2048,3584]{1,0:T(8,128)(2,1)} %param.7), kind=kOutput, calls=%fused_computation.5 | convolution fusion | flops 2818965504 | bytes 19202048 | tf_op jit(solution)/shard_map/dot_general | solution.py:8
  244.9 1.3 copy-done.1
  246.2 7.6 %fusion = bf16[2048,3584]{0,1:T(8,128)(2,1)} fusion(bf16[192,3584]{1,0:T(8,128)(2,1)S(1)} %copy-done.1, bf16[192,2048]{1,0:T(8,128)(2,1)S(1)} %all_gather.15), kind=kOutput, calls=%fused_computation.3 | convolution fusion | flops 2825912320 | bytes 16842752 | tf_op jit(solution)/shard_map/dot_general | solution.py:14
  253.8 18.8 %copy.10 = bf16[2048,3584]{1,0:T(8,128)(2,1)} copy(bf16[2048,3584]{0,1:T(8,128)(2,1)} %fusion) | data formatting | bytes 29360128
  272.6 7.6 %fusion.1 = bf16[2048,3584]{0,1:T(8,128)(2,1)} fusion(bf16[192,3584]{1,0:T(8,128)(2,1)S(1)} %copy-done.2, bf16[192,2048]{1,0:T(8,128)(2,1)S(1)} %all_gather.15), kind=kOutput, calls=%fused_computation.4 | convolution fusion | flops 2825912320 | bytes 16842752 | tf_op jit(solution)/shard_map/dot_general | solution.py:14
  280.2 18.8 %copy.11 = bf16[2048,3584]{1,0:T(8,128)(2,1)} copy(bf16[2048,3584]{0,1:T(8,128)(2,1)} %fusion.1) | data formatting | bytes 29360128
  299.0 7.6 %convolution_convert_fusion = bf16[3584,2048]{1,0:T(8,128)(2,1)} fusion(bf16[192,3584]{1,0:T(8,128)(2,1)S(1)} %copy-done, bf16[192,2048]{1,0:T(8,128)(2,1)S(1)} %all_gather.17), kind=kOutput, calls=%fused_computation | convolution fusion | flops 2825912320 | bytes 16842752 | tf_op jit(solution)/shard_map/dot_general | solution.py:14
  306.6 1.6 convert_element_type.31
  308.2 62.1 %reduce-scatter.14.cloned.1.call-done = f32[24,2048]{1,0:T(8,128)} async-done(((f32[192,2048]{1,0:T(8,128)}), f32[24,2048]{1,0:T(8,128)}) %reduce-scatter.14.cloned.1.call-update) | async-done | bytes 196624 | tf_op jit(solution)/shard_map/reduce_scatter | solution.py:58
  370.3 1.6 convert_element_type.34
  (16 shorter events, 0.2 us)
Async XLA Ops:
  7.2 98.5 %reduce-scatter.12.cloned.1.call-start = ((), (), s32[]{:S(2)}) async-start(), calls=%async_computation.9 | async-start | bytes 3440640 | tf_op jit(solution)/shard_map/reduce_scatter | solution.py:52
  53.0 0.9 copy-start.3
  53.0 79.1 %reduce-scatter.6.cloned.1.call-start = ((), (), s32[]{:S(2)}) async-start(), calls=%async_computation.5 | async-start | bytes 3440640 | tf_op jit(solution)/shard_map/reduce_scatter | solution.py:39
  95.8 74.9 %reduce-scatter.8.cloned.1.call-start = ((), (), s32[]{:S(2)}) async-start(), calls=%async_computation.6 | async-start | bytes 3440640 | tf_op jit(solution)/shard_map/reduce_scatter | solution.py:40
  105.6 86.6 %all-gather.4.cloned.1.call-start = ((), (), s32[]{:S(2)}) async-start(), calls=%async_computation.7 | async-start | bytes 1720320 | tf_op jit(solution)/shard_map/all_gather | solution.py:43
  173.5 39.2 %all-gather.6.cloned.1.call-start = ((), (), s32[]{:S(2)}) async-start(), calls=%async_computation.10 | async-start | bytes 1720320 | tf_op jit(solution)/shard_map/all_gather | solution.py:55
  174.1 59.2 %all-gather.8.cloned.1.call-start = ((), (), s32[]{:S(2)}) async-start(), calls=%async_computation.11 | async-start | bytes 1720320 | tf_op jit(solution)/shard_map/all_gather | solution.py:56
  174.6 132.0 %reduce-scatter.10.cloned.1.call-start = ((), (), s32[]{:S(2)}) async-start(), calls=%async_computation.8 | async-start | bytes 1769472 | tf_op jit(solution)/shard_map/reduce_scatter | solution.py:44
  202.0 168.3 %reduce-scatter.14.cloned.1.call-start = ((), (), s32[]{:S(2)}) async-start(), calls=%async_computation.12 | async-start | bytes 1769472 | tf_op jit(solution)/shard_map/reduce_scatter | solution.py:58
  244.9 1.3 copy-start.1
  253.8 18.8 %copy-start.2 = (bf16[192,3584]{1,0:T(8,128)(2,1)S(1)}, bf16[192,3584]{1,0:T(8,128)(2,1)}, u32[]{:S(2)}) copy-start(bf16[192,3584]{1,0:T(8,128)(2,1)} %all-gather.8.cloned.1.call-done) | copy-start | bytes 4128772
  280.2 18.8 %copy-start = (bf16[192,3584]{1,0:T(8,128)(2,1)S(1)}, bf16[192,3584]{1,0:T(8,128)(2,1)}, u32[]{:S(2)}) copy-start(bf16[192,3584]{1,0:T(8,128)(2,1)} %all-gather.4.cloned.1.call-done) | copy-start | bytes 4128772
Sparse Core Ops, SparseCore 0:
  53.1 36.2 reduce-scatter.11
  95.9 36.1 reduce-scatter.5
  135.3 35.3 reduce-scatter.7
  173.6 18.5 all-gather.3
  194.1 18.5 all-gather.5
  214.7 18.5 all-gather.7
  236.7 65.4 reduce-scatter.9
  305.6 64.6 reduce-scatter.13
where the time goes:
time: 380 us; the launch traced here: 379 us
  waiting for transfers between devices  168 us (44%)
  matrix products  83.8 us (22%)
  blocking collectives  66.2 us (17%)
  local copies, waits for them, and re-layouts  39.7 us (10%)
  between operations  14.2 us (4%)
  other arithmetic  5.93 us (2%)
    reduce_scatter x1, waiting for transfers between devices, shards(): lax.psum_scatter(contract_last(d_gate_all, gate_weight) + contract_last(d...  62.1 us
    unnamed x10, local copies, waits for them, and re-layouts  39.7 us
    reduce_scatter x1, waiting for transfers between devices, shards(): lax.psum_scatter(up_part, 'col', scatter_dimension=0, tiled=True)  38.5 us
    all_gather x1, blocking collectives, shards(): grad_all = lax.all_gather(out_grad, 'row', axis=0, tiled=True)  34.1 us
    all_gather x1, blocking collectives, shards(): inputs_all = lax.all_gather(tokens_in, 'row', axis=0, tiled=True)  32.1 us
    dot_general x3, matrix products, contract_last(): lax.dot_general(left, right, (((1,), (1,)), ((), ())), preferred_element_...  31.8 us
    reduce_scatter x1, waiting for transfers between devices, shards(): lax.psum_scatter(gate_part, 'col', scatter_dimension=0, tiled=True)  26.5 us
    dot_general x3, matrix products, contract_first(): lax.dot_general(left, right, (((0,), (0,)), ((), ())), preferred_element_...  22.8 us
  transfers between devices with their start and end apart: 8, of which 6 were waited for; matrix products, arithmetic and copies ran while one was open for 29% of the time, Pallas kernels for 0%

commit v1 on v0

--- a/solution.py
+++ b/solution.py
@@ -2,6 +2,12 @@
 import jax.numpy as jnp
 from jax import lax
 from jax.sharding import PartitionSpec as P
+
+
+def in_order(blocks, dim):
+    shape = list(blocks.shape[1:])
+    shape[dim] *= blocks.shape[0]
+    return jnp.moveaxis(blocks, 0, dim).reshape(shape)
 
 
 def contract_last(left, right):
@@ -47,7 +53,14 @@
         scatter_dimension=0,
         tiled=True,
     ).astype(jnp.bfloat16)
-    grad_all = lax.all_gather(out_grad, "row", axis=0, tiled=True)
+    length = lax.axis_size("row")
+    route = [(i, (i + 1) % length) for i in range(length)]
+    blocks = [out_grad]
+    while len(blocks) < length:
+        blocks.append(lax.ppermute(blocks[-1], "row", route))
+    index = lax.axis_index("row")
+    blocks = jnp.stack(blocks)[(index - jnp.arange(length)) % length]
+    grad_all = in_order(blocks, 0)
     dhid_part = contract_last(grad_all, down_weight)
     d_hidden = lax.psum_scatter(dhid_part, "col", scatter_dimension=0, tiled=True)
     d_gate, d_up = backward_gate(d_hidden, gate_pre, up_pre, sigma_gate, activated)

time: 380 us -> 374 us (0.984)
  blocking collectives: 66.2 us -> 34.1 us
  waiting for transfers between devices: 168 us -> 192 us
    ppermute x0 -> x7, waiting for transfers between devices: none -> 50.5 us  [shards(): blocks.append(lax.ppermute(blocks[-1], 'row', route))]
    reduce_scatter x1, waiting for transfers between devices: 38.5 us -> 0.02 us  [shards(): lax.psum_scatter(up_part, 'col', scatter_dimension=0, tiled=True)]
    reduce_scatter x1, waiting for transfers between devices: 0.02 us -> 38.1 us  [shards(): lax.psum_scatter(dhid_part, 'col', scatter_dimension=0, tiled=True)]
    all_gather x1 -> x0, blocking collectives: 34.1 us -> none  [shards(): grad_all = lax.all_gather(out_grad, 'row', axis=0, tiled=True)]
    reduce_scatter x1, waiting for transfers between devices: 26.5 us -> 0.02 us  [shards(): lax.psum_scatter(gate_part, 'col', scatter_dimension=0, tiled=True)]
    unnamed x10 -> x17, local copies, waits for them, and re-layouts: 39.7 us -> 39.8 us
  transfers between devices with their start and end apart: 8 -> 15, of which waited for: 6 -> 12; matrix products, arithmetic and copies ran while one was open for 29% -> 31% of each run, Pallas kernels for 0% -> 0%
where the time goes in v1:
time: 374 us; the launch traced here: 373 us
  waiting for transfers between devices  192 us (51%)
  matrix products  83.9 us (22%)
  local copies, waits for them, and re-layouts  40.4 us (11%)
  blocking collectives  34.1 us (9%)
  between operations  14.2 us (4%)
  other arithmetic  5.95 us (2%)
    reduce_scatter x1, waiting for transfers between devices, shards(): lax.psum_scatter(contract_last(d_gate_all, gate_weight) + contract_last(d...  62.2 us
    ppermute x7, waiting for transfers between devices, shards(): blocks.append(lax.ppermute(blocks[-1], 'row', route))  50.5 us
    unnamed x17, local copies, waits for them, and re-layouts  39.8 us
    reduce_scatter x1, waiting for transfers between devices, shards(): lax.psum_scatter(dhid_part, 'col', scatter_dimension=0, tiled=True)  38.1 us
    all_gather x1, blocking collectives, shards(): inputs_all = lax.all_gather(tokens_in, 'row', axis=0, tiled=True)  34.1 us
    dot_general x3, matrix products, contract_last(): lax.dot_general(left, right, (((1,), (1,)), ((), ())), preferred_element_...  31.9 us
    dot_general x3, matrix products, contract_first(): lax.dot_general(left, right, (((0,), (0,)), ((), ())), preferred_element_...  22.8 us
    all_gather x1, waiting for transfers between devices, shards(): hidden_all = lax.all_gather(hidden_share, 'col', axis=0, tiled=True)  17.3 us
  transfers between devices with their start and end apart: 15, of which 12 were waited for; matrix products, arithmetic and copies ran while one was open for 31% of the time, Pallas kernels for 0%

profile of v1, /device:TPU:0, one launch (start us, length us, event | category | flops | bytes accessed | tf_op | source)
XLA Modules:
  0.0 372.6 jit_solution(15795913255214046446)
XLA Ops:
  7.2 34.1 %all_gather.12 = bf16[192,2048]{1,0:T(8,128)(2,1)S(1)} all-gather(bf16[24,2048]{1,0:T(8,128)(2,1)} %param.5), channel_id=1, replica_groups=mesh['row'=8,'col'=4] {'row'}, dimensions={0}, use_global_device_ids=true | all-gather | bytes 884736 | tf_op jit(solution)/shard_map/all_gather | solution.py:41
  41.3 9.7 %fusion.5 = f32[192,3584]{1,0:T(8,128)} fusion(bf16[192,2048]{1,0:T(8,128)(2,1)S(1)} %all_gather.12, bf16[2048,3584]{1,0:T(8,128)(2,1)} %param.6), kind=kOutput, calls=%fused_computation.27 | convolution fusion | flops 2818572288 | bytes 18219008 | tf_op jit(solution)/shard_map/dot_general | solution.py:42
  51.1 9.7 %fusion.6 = f32[192,3584]{1,0:T(8,128)} fusion(bf16[192,2048]{1,0:T(8,128)(2,1)S(1)} %all_gather.12, bf16[2048,3584]{1,0:T(8,128)(2,1)} %param.7), kind=kOutput, calls=%fused_computation.28 | convolution fusion | flops 2818572288 | bytes 18219008 | tf_op jit(solution)/shard_map/dot_general | solution.py:43
  60.9 0.8 copy-done.3
  61.7 1.5 collective-permute-start
  63.3 6.7 %collective-permute-done = bf16[24,2048]{1,0:T(8,128)(2,1)S(1)} collective-permute-done((bf16[24,2048]{1,0:T(8,128)(2,1)S(1)}, bf16[24,2048]{1,0:T(8,128)(2,1)S(1)}, u32[]{:S(2)}, u32[]{:S(2)}) %collective-permute-start) | collective-permute-done | bytes 98336 | tf_op jit(solution)/shard_map/ppermute | solution.py:60
  70.0 7.4 %collective-permute-done.1 = bf16[24,2048]{1,0:T(8,128)(2,1)S(1)} collective-permute-done((bf16[24,2048]{1,0:T(8,128)(2,1)S(1)}, bf16[24,2048]{1,0:T(8,128)(2,1)S(1)}, u32[]{:S(2)}, u32[]{:S(2)}) %collective-permute-start.1) | collective-permute-done | bytes 98336 | tf_op jit(solution)/shard_map/ppermute | solution.py:60
  77.4 7.3 %collective-permute-done.2 = bf16[24,2048]{1,0:T(8,128)(2,1)S(1)} collective-permute-done((bf16[24,2048]{1,0:T(8,128)(2,1)S(1)}, bf16[24,2048]{1,0:T(8,128)(2,1)S(1)}, u32[]{:S(2)}, u32[]{:S(2)}) %collective-permute-start.2) | collective-permute-done | bytes 98336 | tf_op jit(solution)/shard_map/ppermute | solution.py:60
  84.7 7.3 %collective-permute-done.3 = bf16[24,2048]{1,0:T(8,128)(2,1)S(1)} collective-permute-done((bf16[24,2048]{1,0:T(8,128)(2,1)S(1)}, bf16[24,2048]{1,0:T(8,128)(2,1)S(1)}, u32[]{:S(2)}, u32[]{:S(2)}) %collective-permute-start.3) | collective-permute-done | bytes 98336 | tf_op jit(solution)/shard_map/ppermute | solution.py:60
  92.0 7.3 %collective-permute-done.4 = bf16[24,2048]{1,0:T(8,128)(2,1)S(1)} collective-permute-done((bf16[24,2048]{1,0:T(8,128)(2,1)S(1)}, bf16[24,2048]{1,0:T(8,128)(2,1)S(1)}, u32[]{:S(2)}, u32[]{:S(2)}) %collective-permute-start.4) | collective-permute-done | bytes 98336 | tf_op jit(solution)/shard_map/ppermute | solution.py:60
  99.3 7.3 %collective-permute-done.5 = bf16[24,2048]{1,0:T(8,128)(2,1)S(1)} collective-permute-done((bf16[24,2048]{1,0:T(8,128)(2,1)S(1)}, bf16[24,2048]{1,0:T(8,128)(2,1)S(1)}, u32[]{:S(2)}, u32[]{:S(2)}) %collective-permute-start.5) | collective-permute-done | bytes 98336 | tf_op jit(solution)/shard_map/ppermute | solution.py:60
  106.6 7.3 %collective-permute-done.6 = bf16[24,2048]{1,0:T(8,128)(2,1)S(1)} collective-permute-done((bf16[24,2048]{1,0:T(8,128)(2,1)S(1)}, bf16[24,2048]{1,0:T(8,128)(2,1)S(1)}, u32[]{:S(2)}, u32[]{:S(2)}) %collective-permute-start.6) | collective-permute-done | bytes 98336 | tf_op jit(solution)/shard_map/ppermute | solution.py:60
  113.9 0.6 gather_fusion
  114.5 11.8 %fusion.8 = f32[192,3584]{1,0:T(8,128)} fusion(bf16[192,2048]{1,0:T(8,128)(2,1)S(1)} %bitcast.41, bf16[3584,2048]{1,0:T(8,128)(2,1)} %param.8), kind=kOutput, calls=%fused_computation.30 | convolution fusion | flops 2818572288 | bytes 18219008 | tf_op jit(solution)/shard_map/dot_general | solution.py:14
  126.4 38.1 %reduce-scatter.12.cloned.1.call-done = f32[48,3584]{1,0:T(8,128)} async-done(((f32[192,3584]{1,0:T(8,128)}), f32[48,3584]{1,0:T(8,128)}) %reduce-scatter.12.cloned.1.call-update) | async-done | bytes 688144 | tf_op jit(solution)/shard_map/reduce_scatter | solution.py:65
  164.5 2.8 multiply_convert_fusion
  167.3 0.5 all-gather.6.cloned.1.call-update
  168.7 17.3 %all-gather.4.cloned.1.call-done = bf16[192,3584]{1,0:T(8,128)(2,1)} async-done(((bf16[48,3584]{1,0:T(8,128)(2,1)}), bf16[192,3584]{1,0:T(8,128)(2,1)}) %all-gather.4.cloned.1.call-update) | async-done | bytes 1376272 | tf_op jit(solution)/shard_map/all_gather | solution.py:49
  186.0 9.8 %fusion.7 = f32[192,2048]{1,0:T(8,128)} fusion(bf16[192,3584]{1,0:T(8,128)(2,1)} %all-gather.4.cloned.1.call-done, bf16[3584,2048]{1,0:T(8,128)(2,1)} %param.8), kind=kOutput, calls=%fused_computation.29 | convolution fusion | flops 2818572288 | bytes 17629184 | tf_op jit(solution)/shard_map/dot_general | solution.py:51
  195.8 10.7 %all-gather.6.cloned.1.call-done = bf16[192,3584]{1,0:T(8,128)(2,1)} async-done(((bf16[48,3584]{1,0:T(8,128)(2,1)}), bf16[192,3584]{1,0:T(8,128)(2,1)}) %all-gather.6.cloned.1.call-update) | async-done | bytes 1376272 | tf_op jit(solution)/shard_map/all_gather | solution.py:68
  206.5 8.5 %fusion.9 = f32[192,2048]{1,0:T(8,128)S(1)} fusion(bf16[192,3584]{1,0:T(8,128)(2,1)} %all-gather.6.cloned.1.call-done, bf16[2048,3584]{1,0:T(8,128)(2,1)} %param.6), kind=kOutput, calls=%fused_computation.31 | convolution fusion | flops 2818572288 | bytes 17629184 | tf_op jit(solution)/shard_map/dot_general | solution.py:14
  215.0 12.1 %all-gather.8.cloned.1.call-done = bf16[192,3584]{1,0:T(8,128)(2,1)} async-done(((bf16[48,3584]{1,0:T(8,128)(2,1)}), bf16[192,3584]{1,0:T(8,128)(2,1)}) %all-gather.8.cloned.1.call-update) | async-done | bytes 1376272 | tf_op jit(solution)/shard_map/all_gather | solution.py:69
  227.1 11.6 %convolution_add_fusion = f32[192,2048]{1,0:T(8,128)} fusion(f32[192,2048]{1,0:T(8,128)S(1)} %fusion.9, bf16[192,3584]{1,0:T(8,128)(2,1)} %all-gather.8.cloned.1.call-done, bf16[2048,3584]{1,0:T(8,128)(2,1)} %param.7), kind=kOutput, calls=%fused_computation.6 | convolution fusion | flops 2818965504 | bytes 19202048 | tf_op jit(solution)/shard_map/dot_general | solution.py:14
  238.7 1.3 copy-done.1
  240.0 7.6 %fusion = bf16[2048,3584]{0,1:T(8,128)(2,1)} fusion(bf16[192,3584]{1,0:T(8,128)(2,1)S(1)} %copy-done.1, bf16[192,2048]{1,0:T(8,128)(2,1)S(1)} %all_gather.12), kind=kOutput, calls=%fused_computation.4 | convolution fusion | flops 2825912320 | bytes 16842752 | tf_op jit(solution)/shard_map/dot_general | solution.py:20
  247.6 18.9 %copy.10 = bf16[2048,3584]{1,0:T(8,128)(2,1)} copy(bf16[2048,3584]{0,1:T(8,128)(2,1)} %fusion) | data formatting | bytes 29360128
  266.5 7.6 %fusion.1 = bf16[2048,3584]{0,1:T(8,128)(2,1)} fusion(bf16[192,3584]{1,0:T(8,128)(2,1)S(1)} %copy-done.2, bf16[192,2048]{1,0:T(8,128)(2,1)S(1)} %all_gather.12), kind=kOutput, calls=%fused_computation.5 | convolution fusion | flops 2825912320 | bytes 16842752 | tf_op jit(solution)/shard_map/dot_general | solution.py:20
  274.1 18.8 %copy.11 = bf16[2048,3584]{1,0:T(8,128)(2,1)} copy(bf16[2048,3584]{0,1:T(8,128)(2,1)} %fusion.1) | data formatting | bytes 29360128
  292.8 7.6 %convolution_convert_fusion = bf16[3584,2048]{1,0:T(8,128)(2,1)} fusion(bf16[192,3584]{1,0:T(8,128)(2,1)S(1)} %copy-done, bf16[192,2048]{1,0:T(8,128)(2,1)S(1)} %bitcast.42), kind=kOutput, calls=%fused_computation.1 | convolution fusion | flops 2825912320 | bytes 16842752 | tf_op jit(solution)/shard_map/dot_general | solution.py:20
  300.4 1.6 convert_element_type.31
  302.0 62.2 %reduce-scatter.14.cloned.1.call-done = f32[24,2048]{1,0:T(8,128)} async-done(((f32[192,2048]{1,0:T(8,128)}), f32[24,2048]{1,0:T(8,128)}) %reduce-scatter.14.cloned.1.call-update) | async-done | bytes 196624 | tf_op jit(solution)/shard_map/reduce_scatter | solution.py:71
  364.2 1.6 convert_element_type.34
  (40 shorter events, 1.3 us)
Async XLA Ops:
  7.2 119.2 %reduce-scatter.6.cloned.1.call-start = ((), (), s32[]{:S(2)}) async-start(), calls=%async_computation.5 | async-start | bytes 3440640 | tf_op jit(solution)/shard_map/reduce_scatter | solution.py:45
  51.0 75.4 %reduce-scatter.8.cloned.1.call-start = ((), (), s32[]{:S(2)}) async-start(), calls=%async_computation.6 | async-start | bytes 3440640 | tf_op jit(solution)/shard_map/reduce_scatter | solution.py:46
  60.8 0.9 copy-start.3
  60.8 103.7 %reduce-scatter.12.cloned.1.call-start = ((), (), s32[]{:S(2)}) async-start(), calls=%async_computation.9 | async-start | bytes 3440640 | tf_op jit(solution)/shard_map/reduce_scatter | solution.py:65
  61.7 8.2 %collective-permute-start = (bf16[24,2048]{1,0:T(8,128)(2,1)S(1)}, bf16[24,2048]{1,0:T(8,128)(2,1)S(1)}, u32[]{:S(2)}, u32[]{:S(2)}) collective-permute-start(bf16[24,2048]{1,0:T(8,128)(2,1)S(1)} %copy-done.3), channel_id=1, source_target_pairs={{0,4},{4,8},{8,12},{12,16},{16,20},{20,24},{24,28},{28,0},{1,5},{5... | collective-permute-start | bytes 294920 | tf_op jit(solution)/shard_map/ppermute | solution.py:60
  70.0 7.4 %collective-permute-start.1 = (bf16[24,2048]{1,0:T(8,128)(2,1)S(1)}, bf16[24,2048]{1,0:T(8,128)(2,1)S(1)}, u32[]{:S(2)}, u32[]{:S(2)}) collective-permute-start(bf16[24,2048]{1,0:T(8,128)(2,1)S(1)} %collective-permute-done), channel_id=1, source_target_pairs={{0,4},{4,8},{8,12},{12,16},{16,20},{20,24},{24,28},{28,0},{1,5},{5... | collective-permute-start | bytes 294920 | tf_op jit(solution)/shard_map/ppermute | solution.py:60
  77.3 7.3 %collective-permute-start.2 = (bf16[24,2048]{1,0:T(8,128)(2,1)S(1)}, bf16[24,2048]{1,0:T(8,128)(2,1)S(1)}, u32[]{:S(2)}, u32[]{:S(2)}) collective-permute-start(bf16[24,2048]{1,0:T(8,128)(2,1)S(1)} %collective-permute-done.1), channel_id=1, source_target_pairs={{0,4},{4,8},{8,12},{12,16},{16,20},{20,24},{24,28},{28,0},{1,5},{5... | collective-permute-start | bytes 294920 | tf_op jit(solution)/shard_map/ppermute | solution.py:60
  84.7 7.3 %collective-permute-start.3 = (bf16[24,2048]{1,0:T(8,128)(2,1)S(1)}, bf16[24,2048]{1,0:T(8,128)(2,1)S(1)}, u32[]{:S(2)}, u32[]{:S(2)}) collective-permute-start(bf16[24,2048]{1,0:T(8,128)(2,1)S(1)} %collective-permute-done.2), channel_id=1, source_target_pairs={{0,4},{4,8},{8,12},{12,16},{16,20},{20,24},{24,28},{28,0},{1,5},{5... | collective-permute-start | bytes 294920 | tf_op jit(solution)/shard_map/ppermute | solution.py:60
  92.0 7.3 %collective-permute-start.4 = (bf16[24,2048]{1,0:T(8,128)(2,1)S(1)}, bf16[24,2048]{1,0:T(8,128)(2,1)S(1)}, u32[]{:S(2)}, u32[]{:S(2)}) collective-permute-start(bf16[24,2048]{1,0:T(8,128)(2,1)S(1)} %collective-permute-done.3), channel_id=1, source_target_pairs={{0,4},{4,8},{8,12},{12,16},{16,20},{20,24},{24,28},{28,0},{1,5},{5... | collective-permute-start | bytes 294920 | tf_op jit(solution)/shard_map/ppermute | solution.py:60
  99.3 7.3 %collective-permute-start.5 = (bf16[24,2048]{1,0:T(8,128)(2,1)S(1)}, bf16[24,2048]{1,0:T(8,128)(2,1)S(1)}, u32[]{:S(2)}, u32[]{:S(2)}) collective-permute-start(bf16[24,2048]{1,0:T(8,128)(2,1)S(1)} %collective-permute-done.4), channel_id=1, source_target_pairs={{0,4},{4,8},{8,12},{12,16},{16,20},{20,24},{24,28},{28,0},{1,5},{5... | collective-permute-start | bytes 294920 | tf_op jit(solution)/shard_map/ppermute | solution.py:60
  106.6 7.3 %collective-permute-start.6 = (bf16[24,2048]{1,0:T(8,128)(2,1)S(1)}, bf16[24,2048]{1,0:T(8,128)(2,1)S(1)}, u32[]{:S(2)}, u32[]{:S(2)}) collective-permute-start(bf16[24,2048]{1,0:T(8,128)(2,1)S(1)} %collective-permute-done.5), channel_id=1, source_target_pairs={{0,4},{4,8},{8,12},{12,16},{16,20},{20,24},{24,28},{28,0},{1,5},{5... | collective-permute-start | bytes 294920 | tf_op jit(solution)/shard_map/ppermute | solution.py:60
  126.3 59.6 %all-gather.4.cloned.1.call-start = ((), (), s32[]{:S(2)}) async-start(), calls=%async_computation.7 | async-start | bytes 1720320 | tf_op jit(solution)/shard_map/all_gather | solution.py:49
  167.3 39.2 %all-gather.6.cloned.1.call-start = ((), (), s32[]{:S(2)}) async-start(), calls=%async_computation.10 | async-start | bytes 1720320 | tf_op jit(solution)/shard_map/all_gather | solution.py:68
  167.9 59.2 %all-gather.8.cloned.1.call-start = ((), (), s32[]{:S(2)}) async-start(), calls=%async_computation.11 | async-start | bytes 1720320 | tf_op jit(solution)/shard_map/all_gather | solution.py:69
  168.5 132.0 %reduce-scatter.10.cloned.1.call-start = ((), (), s32[]{:S(2)}) async-start(), calls=%async_computation.8 | async-start | bytes 1769472 | tf_op jit(solution)/shard_map/reduce_scatter | solution.py:50
  195.8 168.4 %reduce-scatter.14.cloned.1.call-start = ((), (), s32[]{:S(2)}) async-start(), calls=%async_computation.12 | async-start | bytes 1769472 | tf_op jit(solution)/shard_map/reduce_scatter | solution.py:71
  238.7 1.3 copy-start.1
  247.6 18.9 %copy-start.2 = (bf16[192,3584]{1,0:T(8,128)(2,1)S(1)}, bf16[192,3584]{1,0:T(8,128)(2,1)}, u32[]{:S(2)}) copy-start(bf16[192,3584]{1,0:T(8,128)(2,1)} %all-gather.8.cloned.1.call-done) | copy-start | bytes 4128772
  274.1 18.8 %copy-start = (bf16[192,3584]{1,0:T(8,128)(2,1)S(1)}, bf16[192,3584]{1,0:T(8,128)(2,1)}, u32[]{:S(2)}) copy-start(bf16[192,3584]{1,0:T(8,128)(2,1)} %all-gather.4.cloned.1.call-done) | copy-start | bytes 4128772
Sparse Core Ops, SparseCore 0:
  51.2 36.2 reduce-scatter.5
  90.6 35.3 reduce-scatter.7
  129.1 35.3 reduce-scatter.11
  167.4 18.5 all-gather.3
  188.0 18.5 all-gather.5
  208.5 18.5 all-gather.7
  230.5 65.7 reduce-scatter.9
  299.7 64.4 reduce-scatter.13
